TPU v7x, 256 devices: a whole 4x4x8 slice. The times are simulated.
256 devices in a mesh: row: 32 (over x, y, core), col: 8 (over z).
Axes of the slice: x: 4, y: 4, z: 8, core: 2. Of those that a mesh axis runs over, the one named last changes fastest.
Arguments:
- block_values: bfloat16 [32, 8, 192, 128, 128], P('row', 'col'), may hold values from -0.0625 to 0.0625
- block_rows: int32 [32, 8, 192], P('row', 'col'), may hold values from 0 to 4095, as said below
- block_cols: int32 [32, 8, 192], P('row', 'col'), may hold values from 0 to 4095, as said below
- block_counts: int32 [32, 8], P('row', 'col'), may hold values from 48 to 192, as said below
- precond: float32 [8, 512, 128, 128], P('col', 'row')
- right_side: float32 [8, 512, 32, 128], P('col', 'row'), may hold values from -6 to 6
Outputs:
- solution: float32 [8, 512, 32, 128], P('col', 'row')
Inputs may be any that keep to these rules, and one draw needn't show every extreme that they name: `block_rows`: the block rows of device (r, c) lie in [c * 512, (c + 1) * 512); positions may repeat; for each j, at most 9 of a device's 192 slots have (row mod 512) // 16 == j, and in every index of col some j has exactly 9 such slots on every device. `block_cols`: every block column q of device (r, c) has (q mod 512) // 16 == r; positions may repeat. `block_counts`: slots at or past a device's count are unused; some device uses all 192 slots.
All inputs are finite; a program needn't handle non-finite values.
Results may differ from a plain program's by a relative error of at most 0.00073.
Values may be sent and summed in bfloat16 or wider, within the bound.
A program may use at most 64 MiB of HBM per device.

v0:
```python
import jax
import jax.numpy as jnp
from jax import lax
from jax.sharding import PartitionSpec as P

ITERS = 3


def apply_blocks(matrix, field):
    return jnp.einsum("poi,pki->pko", matrix, field, precision=lax.Precision.HIGHEST)


def block_terms(vectors, values, col_local):
    gathered = vectors[col_local]
    return jnp.einsum("ski,soi->sko", gathered, values, preferred_element_type=jnp.float32)


def per_device(block_values, block_rows, block_cols, block_counts, precond, right_side):
    owned = right_side.shape[1]
    row_devices = lax.axis_size("row")
    group = owned * row_devices
    slot_total = block_values.shape[2]
    values = block_values[0, 0]
    row_local = block_rows[0, 0] % group
    col_global = block_cols[0, 0]
    col_local = col_global // group * owned + col_global % owned
    used = block_counts[0, 0]
    live = jnp.arange(slot_total, dtype=jnp.int32) < used
    inverse = precond[0]
    rhs_own = right_side[0]
    solution = apply_blocks(inverse, rhs_own)
    for step in range(ITERS):
        pieces = lax.all_gather(solution.astype(jnp.bfloat16)[None], "col", axis=1, tiled=True)[0]
        terms = block_terms(pieces, values, col_local)
        terms = jnp.where(live[:, None, None], terms, jnp.zeros_like(terms))
        partial_value = jax.ops.segment_sum(terms, row_local, num_segments=group)
        product = lax.psum_scatter(partial_value, "row", scatter_dimension=0, tiled=True)
        residual = rhs_own - solution - product
        solution = solution + apply_blocks(inverse, residual)
    return solution[None]


def solution(mesh):
    placed = (
        P("row", "col", None, None, None),
        P("row", "col", None),
        P("row", "col", None),
        P("row", "col"),
        P("col", "row", None, None),
        P("col", "row", None, None),
    )
    return jax.shard_map(
        per_device,
        mesh=mesh,
        in_specs=placed,
        out_specs=P("col", "row", None, None),
        check_vma=False,
    )
```

profile of v0, /device:TPU:2, one launch (start us, length us, event | category | flops | bytes accessed | tf_op | source)
XLA Modules:
  0.0 562.6 jit_solution(1981962366836233417)
XLA Ops:
  6.5 0.0 copy-start
  6.5 0.0 all-gather.7.cloned.1.call-start
  6.5 1.2 copy-done
  7.8 3.3 fusion.30
  11.1 0.0 all-gather.7.cloned.1.call-update
  11.1 0.0 reduce-scatter.4.cloned.1.call-start
  11.8 0.7 compare_select_fusion
  12.5 0.7 and_select_fusion.2
  13.2 39.4 %all-gather.7.cloned.1.call-done = bf16[128,32,128]{2,1,0:T(8,128)(2,1)} async-done(((bf16[16,32,128]{2,1,0:T(8,128)(2,1)}), bf16[128,32,128]{2,1,0:T(8,128)(2,1)}) %all-gather.7.cloned.1.call-update) | async-done | bytes 1048592 | tf_op jit(solution)/shard_map/all_gather | solution.py:33
  52.6 2.1 gather_fusion
  54.8 7.9 %fusion.6 = f32[192,32,128]{2,1,0:T(8,128)} fusion(bf16[192,32,128]{2,1,0:T(8,128)(2,1)S(1)} %gather_fusion, bf16[1,1,192,128,128]{4,3,2,1,0:T(8,128)(2,1)} %param.6, pred[192]{0:T(512)(128)(4,1)S(1)} %iota_compare_fusion), kind=kOutput, calls=%fused_computation.12 | convolution fusion | flops 202113024 | bytes 11010240 | tf_op jit(solution)/shard_map/ski,soi->sko/dot_general | solution.py:15
  62.7 4.3 broadcast.156.clone
  67.0 25.8 %scatter_fusion = f32[512,32,128]{2,1,0:T(8,128)} fusion(f32[512,32,128]{2,1,0:T(8,128)} %broadcast.156.clone, s32[192]{0:T(256)S(1)} %bitcast.73, f32[192,32,128]{2,1,0:T(8,128)} %fusion.6), kind=kCustom, calls=%fused_computation.3 | custom fusion | flops 786432 | bytes 9437952 | tf_op jit(solution)/shard_map/scatter-add | solution.py:36
  92.8 0.0 copy-start.1
  92.8 0.0 reduce-scatter.4.cloned.1.call-update
  92.9 0.0 all-gather.9.cloned.1.call-start
  92.9 98.6 %reduce-scatter.4.cloned.1.call-done = f32[16,32,128]{2,1,0:T(8,128)} async-done(((f32[512,32,128]{2,1,0:T(8,128)}), f32[16,32,128]{2,1,0:T(8,128)}) %reduce-scatter.4.cloned.1.call-update) | async-done | bytes 262160 | tf_op jit(solution)/shard_map/reduce_scatter | solution.py:37
  191.5 0.0 copy-done.1
  191.5 3.3 fusion.31
  194.8 0.0 all-gather.9.cloned.1.call-update
  194.8 0.0 reduce-scatter.6.cloned.1.call-start
  194.9 38.2 %all-gather.9.cloned.1.call-done = bf16[128,32,128]{2,1,0:T(8,128)(2,1)} async-done(((bf16[16,32,128]{2,1,0:T(8,128)(2,1)}), bf16[128,32,128]{2,1,0:T(8,128)(2,1)}) %all-gather.9.cloned.1.call-update) | async-done | bytes 1048592 | tf_op jit(solution)/shard_map/all_gather | solution.py:33
  233.1 2.1 gather_fusion.1
  235.2 7.9 %fusion.9 = f32[192,32,128]{2,1,0:T(8,128)} fusion(bf16[192,32,128]{2,1,0:T(8,128)(2,1)S(1)} %gather_fusion.1, bf16[1,1,192,128,128]{4,3,2,1,0:T(8,128)(2,1)} %param.6, pred[192]{0:T(512)(128)(4,1)S(1)} %iota_compare_fusion), kind=kOutput, calls=%fused_computation.13 | convolution fusion | flops 202113024 | bytes 11010240 | tf_op jit(solution)/shard_map/ski,soi->sko/dot_general | solution.py:15
  243.1 4.3 broadcast.156.clone.1
  247.4 25.8 %scatter_fusion.1 = f32[512,32,128]{2,1,0:T(8,128)} fusion(f32[512,32,128]{2,1,0:T(8,128)} %broadcast.156.clone.1, s32[192]{0:T(256)S(1)} %bitcast.74, f32[192,32,128]{2,1,0:T(8,128)} %fusion.9), kind=kCustom, calls=%fused_computation.4 | custom fusion | flops 786432 | bytes 9437952 | tf_op jit(solution)/shard_map/scatter-add | solution.py:36
  273.3 0.0 reduce-scatter.6.cloned.1.call-update
  273.3 0.0 all-gather.11.cloned.1.call-start
  273.4 98.6 %reduce-scatter.6.cloned.1.call-done = f32[16,32,128]{2,1,0:T(8,128)} async-done(((f32[512,32,128]{2,1,0:T(8,128)}), f32[16,32,128]{2,1,0:T(8,128)}) %reduce-scatter.6.cloned.1.call-update) | async-done | bytes 262160 | tf_op jit(solution)/shard_map/reduce_scatter | solution.py:37
  371.9 3.3 fusion.32
  375.3 0.0 all-gather.11.cloned.1.call-update
  375.3 0.2 reduce-scatter.8.cloned.1.call-start
  375.5 38.0 %all-gather.11.cloned.1.call-done = bf16[128,32,128]{2,1,0:T(8,128)(2,1)} async-done(((bf16[16,32,128]{2,1,0:T(8,128)(2,1)}), bf16[128,32,128]{2,1,0:T(8,128)(2,1)}) %all-gather.11.cloned.1.call-update) | async-done | bytes 1048592 | tf_op jit(solution)/shard_map/all_gather | solution.py:33
  413.6 2.1 gather_fusion.2
  415.7 7.9 %fusion.12 = f32[192,32,128]{2,1,0:T(8,128)} fusion(bf16[192,32,128]{2,1,0:T(8,128)(2,1)S(1)} %gather_fusion.2, bf16[1,1,192,128,128]{4,3,2,1,0:T(8,128)(2,1)} %param.6, pred[192]{0:T(512)(128)(4,1)S(1)} %iota_compare_fusion), kind=kOutput, calls=%fused_computation.14 | convolution fusion | flops 202113024 | bytes 11010240 | tf_op jit(solution)/shard_map/ski,soi->sko/dot_general | solution.py:15
  423.6 4.3 broadcast.156
  427.9 25.8 %scatter_fusion.2 = f32[512,32,128]{2,1,0:T(8,128)} fusion(f32[512,32,128]{2,1,0:T(8,128)} %broadcast.156, s32[192]{0:T(256)S(1)} %bitcast.75, f32[192,32,128]{2,1,0:T(8,128)} %fusion.12), kind=kCustom, calls=%fused_computation.5 | custom fusion | flops 786432 | bytes 9437952 | tf_op jit(solution)/shard_map/scatter-add | solution.py:36
  453.7 0.0 reduce-scatter.8.cloned.1.call-update
  453.8 98.6 %reduce-scatter.8.cloned.1.call-done = f32[16,32,128]{2,1,0:T(8,128)} async-done(((f32[512,32,128]{2,1,0:T(8,128)}), f32[16,32,128]{2,1,0:T(8,128)}) %reduce-scatter.8.cloned.1.call-update) | async-done | bytes 262160 | tf_op jit(solution)/shard_map/reduce_scatter | solution.py:37
  552.4 3.4 fusion.15
  (2 shorter events, 0.0 us)
Async XLA Ops:
  6.5 1.2 copy-start
  6.5 46.1 %all-gather.7.cloned.1.call-start = ((), (), s32[]{:S(2)}) async-start(), calls=%async_computation.6 | async-start | bytes 1179648 | tf_op jit(solution)/shard_map/all_gather | solution.py:33
  11.1 180.3 %reduce-scatter.4.cloned.1.call-start = ((), (), s32[]{:S(2)}) async-start(), calls=%async_computation.3 | async-start | bytes 8650752 | tf_op jit(solution)/shard_map/reduce_scatter | solution.py:37
  92.8 98.7 %copy-start.1 = (f32[1,16,32,128]{3,2,1,0:T(8,128)S(1)}, f32[1,16,32,128]{3,2,1,0:T(8,128)}, u32[]{:S(2)}) copy-start(f32[1,16,32,128]{3,2,1,0:T(8,128)} %param.11) | copy-start | bytes 786436
  92.9 140.3 %all-gather.9.cloned.1.call-start = ((), (), s32[]{:S(2)}) async-start(), calls=%async_computation.7 | async-start | bytes 1179648 | tf_op jit(solution)/shard_map/all_gather | solution.py:33
  194.8 177.1 %reduce-scatter.6.cloned.1.call-start = ((), (), s32[]{:S(2)}) async-start(), calls=%async_computation.4 | async-start | bytes 8650752 | tf_op jit(solution)/shard_map/reduce_scatter | solution.py:37
  273.3 140.3 %all-gather.11.cloned.1.call-start = ((), (), s32[]{:S(2)}) async-start(), calls=%async_computation.8 | async-start | bytes 1179648 | tf_op jit(solution)/shard_map/all_gather | solution.py:33
  375.3 177.1 %reduce-scatter.8.cloned.1.call-start = ((), (), s32[]{:S(2)}) async-start(), calls=%async_computation.5 | async-start | bytes 8650752 | tf_op jit(solution)/shard_map/reduce_scatter | solution.py:37
Sparse Core Ops, SparseCore 0:
  11.2 41.3 all-gather.6
  93.0 98.4 reduce-scatter.3
  195.0 38.0 all-gather.8
  273.4 98.4 reduce-scatter.5
  375.4 38.0 all-gather.10
  453.9 98.4 reduce-scatter.7
where the time goes:
time: 564 us; the launch traced here: 563 us
  waiting for transfers between devices  412 us (73%)
  other arithmetic  78.9 us (14%)
  matrix products  37.1 us (7%)
  local copies, waits for them, and re-layouts  20.5 us (4%)
  between operations  14.2 us (3%)
    reduce_scatter x3, waiting for transfers between devices, per_device(): lax.psum_scatter(partial_value, 'row', scatter_dimension=0, tiled=True)  296 us
    all_gather x3, waiting for transfers between devices, per_device(): lax.all_gather(solution.astype(jnp.bfloat16)[None], 'col', axis=1, tiled=...  116 us
    scatter-add x3, other arithmetic, per_device(): partial_value = jax.ops.segment_sum(terms, row_local, num_segments=group)  77.5 us
    dot_general x3, matrix products, block_terms(): jnp.einsum('ski,soi->sko', gathered, values, preferred_element_type=jnp.f...  23.7 us
    dot_general x4, matrix products, apply_blocks(): jnp.einsum('poi,pki->pko', matrix, field, precision=lax.Precision.HIGHEST)  13.4 us
    another operation x3, local copies, waits for them, and re-layouts  12.9 us
  transfers between devices with their start and end apart: 6, of which 6 were waited for; matrix products, arithmetic and copies ran while one was open for 0% of the time, Pallas kernels for 0%

commit v1 on v0

--- a/solution.py
+++ b/solution.py
@@ -4,6 +4,11 @@
 from jax.sharding import PartitionSpec as P
 
 ITERS = 3
+
+
+def gather_by_exchange(shard, axis, dim):
+    copies = jnp.concatenate([shard] * lax.axis_size(axis), axis=dim)
+    return lax.all_to_all(copies, axis, dim, dim, tiled=True)
 
 
 def apply_blocks(matrix, field):
@@ -30,7 +35,7 @@
     rhs_own = right_side[0]
     solution = apply_blocks(inverse, rhs_own)
     for step in range(ITERS):
-        pieces = lax.all_gather(solution.astype(jnp.bfloat16)[None], "col", axis=1, tiled=True)[0]
+        pieces = gather_by_exchange(solution.astype(jnp.bfloat16)[None], "col", 1)[0]
         terms = block_terms(pieces, values, col_local)
         terms = jnp.where(live[:, None, None], terms, jnp.zeros_like(terms))
         partial_value = jax.ops.segment_sum(terms, row_local, num_segments=group)

time: 564 us -> 545 us (0.966)
  waiting for transfers between devices: 412 us -> 314 us
  blocking collectives: 0 us -> 66.8 us
  starting transfers between devices: 0.39 us -> 8.59 us
    all_gather x3 -> x0, waiting for transfers between devices: 116 us -> none  [per_device(): lax.all_gather(solution.astype(jnp.bfloat16)[None], 'col', axis=1, tiled=...]
    all_to_all x0 -> x2, blocking collectives: none -> 66.8 us  [gather_by_exchange(): return lax.all_to_all(copies, axis, dim, dim, tiled=True)]
    all_to_all x0 -> x1, waiting for transfers between devices: none -> 28 us  [gather_by_exchange(): return lax.all_to_all(copies, axis, dim, dim, tiled=True)]
    reduce_scatter x3, waiting for transfers between devices: 296 us -> 286 us  [per_device(): lax.psum_scatter(partial_value, 'row', scatter_dimension=0, tiled=True)]
    all_to_all x0 -> x1, starting transfers between devices: none -> 8.47 us  [gather_by_exchange(): return lax.all_to_all(copies, axis, dim, dim, tiled=True)]
  transfers between devices with their start and end apart: 6 -> 4, of which waited for: 6 -> 4; matrix products, arithmetic and copies ran while one was open for 0% -> 0% of each run, Pallas kernels for 0% -> 0%
where the time goes in v1:
time: 545 us; the launch traced here: 544 us
  waiting for transfers between devices  314 us (58%)
  other arithmetic  77.5 us (14%)
  blocking collectives  66.8 us (12%)
  matrix products  37.4 us (7%)
  local copies, waits for them, and re-layouts  25 us (5%)
  between operations  13.9 us (3%)
  starting transfers between devices  8.59 us (2%)
    reduce_scatter x3, waiting for transfers between devices, per_device(): lax.psum_scatter(partial_value, 'row', scatter_dimension=0, tiled=True)  286 us
    scatter-add x3, other arithmetic, per_device(): partial_value = jax.ops.segment_sum(terms, row_local, num_segments=group)  77.5 us
    all_to_all x2, blocking collectives, gather_by_exchange(): return lax.all_to_all(copies, axis, dim, dim, tiled=True)  66.8 us
    all_to_all x1, waiting for transfers between devices, gather_by_exchange(): return lax.all_to_all(copies, axis, dim, dim, tiled=True)  28 us
    dot_general x3, matrix products, block_terms(): jnp.einsum('ski,soi->sko', gathered, values, preferred_element_type=jnp.f...  25.3 us
    another operation x3, local copies, waits for them, and re-layouts  12.9 us
    dot_general x4, matrix products, apply_blocks(): jnp.einsum('poi,pki->pko', matrix, field, precision=lax.Precision.HIGHEST)  12.1 us
  transfers between devices with their start and end apart: 4, of which 4 were waited for; matrix products, arithmetic and copies ran while one was open for 0% of the time, Pallas kernels for 0%

profile of v1, /device:TPU:2, one launch (start us, length us, event | category | flops | bytes accessed | tf_op | source)
XLA Modules:
  0.0 543.6 jit_solution(14811353396795390004)
XLA Ops:
  6.5 0.0 copy-start
  6.5 0.0 copy-start.2
  6.5 0.0 copy-start.3
  6.5 1.2 copy-done
  7.8 3.3 bitcast_dynamic-update-slice_fusion.22
  11.1 0.7 bitcast_dynamic-update-slice_fusion.21
  11.8 0.7 bitcast_dynamic-update-slice_fusion.20
  12.4 0.6 bitcast_dynamic-update-slice_fusion.19
  13.1 0.7 bitcast_dynamic-update-slice_fusion.18
  13.7 0.7 bitcast_dynamic-update-slice_fusion.17
  14.4 0.7 bitcast_dynamic-update-slice_fusion.16
  15.1 0.7 bitcast_dynamic-update-slice_fusion.23
  15.7 8.5 %all-to-all-start = ((bf16[1,128,32,128]{3,2,0,1:T(8,128)(2,1)}), bf16[1,128,32,128]{3,2,0,1:T(8,128)(2,1)S(1)}, u32[]{:S(2)}, u32[]{:S(2)}) async-start(bf16[1,128,32,128]{3,2,0,1:T(8,128)(2,1)} %bitcast.6), calls=%async_computation | async-start | bytes 2097152 | tf_op jit(solution)/shard_map/all_to_all | solution.py:11
  24.2 0.0 reduce-scatter.4.cloned.1.call-start
  24.9 0.0 copy-done.2
  25.0 0.0 copy-done.3
  25.0 28.0 %all-to-all-done = bf16[1,128,32,128]{3,2,0,1:T(8,128)(2,1)S(1)} async-done(((bf16[1,128,32,128]{3,2,0,1:T(8,128)(2,1)}), bf16[1,128,32,128]{3,2,0,1:T(8,128)(2,1)S(1)}, u32[]{:S(2)}, u32[]{:S(2)}) %all-to-all-start) | async-done | bytes 1048608 | tf_op jit(solution)/shard_map/all_to_all | solution.py:11
  52.9 2.0 gather_fusion
  54.9 8.4 %fusion.6 = f32[192,32,128]{2,1,0:T(8,128)} fusion(bf16[192,32,128]{2,1,0:T(8,128)(2,1)} %gather_fusion, bf16[1,1,192,128,128]{4,3,2,1,0:T(8,128)(2,1)} %param.6, pred[192]{0:T(512)(128)(4,1)S(1)} %iota_compare_fusion), kind=kOutput, calls=%fused_computation.12 | convolution fusion | flops 202113024 | bytes 11010240 | tf_op jit(solution)/shard_map/ski,soi->sko/dot_general | solution.py:20
  63.4 4.3 broadcast.156.clone
  67.7 25.8 %scatter_fusion = f32[512,32,128]{2,1,0:T(8,128)} fusion(f32[512,32,128]{2,1,0:T(8,128)} %broadcast.156.clone, s32[192]{0:T(256)S(1)} %bitcast.111, f32[192,32,128]{2,1,0:T(8,128)} %fusion.6), kind=kCustom, calls=%fused_computation.3 | custom fusion | flops 786432 | bytes 9437952 | tf_op jit(solution)/shard_map/scatter-add | solution.py:41
  93.5 0.0 copy-start.1
  93.5 0.0 reduce-scatter.4.cloned.1.call-update
  93.5 0.0 reduce-scatter.6.cloned.1.call-start
  93.6 96.6 %reduce-scatter.4.cloned.1.call-done = f32[16,32,128]{2,1,0:T(8,128)} async-done(((f32[512,32,128]{2,1,0:T(8,128)}), f32[16,32,128]{2,1,0:T(8,128)}) %reduce-scatter.4.cloned.1.call-update) | async-done | bytes 262160 | tf_op jit(solution)/shard_map/reduce_scatter | solution.py:42
  190.1 0.0 copy-done.1
  190.1 2.7 bitcast_dynamic-update-slice_fusion.14
  193.0 33.5 %all_to_all.15 = bf16[1,128,32,128]{3,2,0,1:T(8,128)(2,1)S(1)} all-to-all(bf16[1,128,32,128]{3,2,0,1:T(8,128)(2,1)S(1)} %bitcast.109), channel_id=1, replica_groups=mesh['row'=32,'col'=8] {'col'}, dimensions={1} | all-to-all | bytes 2097152 | tf_op jit(solution)/shard_map/all_to_all | solution.py:11
  226.5 2.0 gather_fusion.1
  228.5 8.4 %fusion.9 = f32[192,32,128]{2,1,0:T(8,128)} fusion(bf16[192,32,128]{2,1,0:T(8,128)(2,1)} %gather_fusion.1, bf16[1,1,192,128,128]{4,3,2,1,0:T(8,128)(2,1)} %param.6, pred[192]{0:T(512)(128)(4,1)S(1)} %iota_compare_fusion), kind=kOutput, calls=%fused_computation.13 | convolution fusion | flops 202113024 | bytes 11010240 | tf_op jit(solution)/shard_map/ski,soi->sko/dot_general | solution.py:20
  236.9 4.3 broadcast.156.clone.1
  241.2 25.8 %scatter_fusion.1 = f32[512,32,128]{2,1,0:T(8,128)} fusion(f32[512,32,128]{2,1,0:T(8,128)} %broadcast.156.clone.1, s32[192]{0:T(256)S(1)} %bitcast.112, f32[192,32,128]{2,1,0:T(8,128)} %fusion.9), kind=kCustom, calls=%fused_computation.4 | custom fusion | flops 786432 | bytes 9437952 | tf_op jit(solution)/shard_map/scatter-add | solution.py:41
  267.0 0.0 reduce-scatter.6.cloned.1.call-update
  267.0 0.0 reduce-scatter.8.cloned.1.call-start
  267.1 94.8 %reduce-scatter.6.cloned.1.call-done = f32[16,32,128]{2,1,0:T(8,128)} async-done(((f32[512,32,128]{2,1,0:T(8,128)}), f32[16,32,128]{2,1,0:T(8,128)}) %reduce-scatter.6.cloned.1.call-update) | async-done | bytes 262160 | tf_op jit(solution)/shard_map/reduce_scatter | solution.py:42
  361.9 2.7 bitcast_dynamic-update-slice_fusion.6
  364.8 33.4 %all_to_all.16 = bf16[1,128,32,128]{3,2,0,1:T(8,128)(2,1)S(1)} all-to-all(bf16[1,128,32,128]{3,2,0,1:T(8,128)(2,1)S(1)} %bitcast.110), channel_id=1, replica_groups=mesh['row'=32,'col'=8] {'col'}, dimensions={1} | all-to-all | bytes 2097152 | tf_op jit(solution)/shard_map/all_to_all | solution.py:11
  398.1 2.0 gather_fusion.2
  400.2 8.4 %fusion.12 = f32[192,32,128]{2,1,0:T(8,128)} fusion(bf16[192,32,128]{2,1,0:T(8,128)(2,1)} %gather_fusion.2, bf16[1,1,192,128,128]{4,3,2,1,0:T(8,128)(2,1)} %param.6, pred[192]{0:T(512)(128)(4,1)S(1)} %iota_compare_fusion), kind=kOutput, calls=%fused_computation.14 | convolution fusion | flops 202113024 | bytes 11010240 | tf_op jit(solution)/shard_map/ski,soi->sko/dot_general | solution.py:20
  408.6 4.3 broadcast.156
  412.9 25.8 %scatter_fusion.2 = f32[512,32,128]{2,1,0:T(8,128)} fusion(f32[512,32,128]{2,1,0:T(8,128)} %broadcast.156, s32[192]{0:T(256)S(1)} %bitcast.113, f32[192,32,128]{2,1,0:T(8,128)} %fusion.12), kind=kCustom, calls=%fused_computation.5 | custom fusion | flops 786432 | bytes 9437952 | tf_op jit(solution)/shard_map/scatter-add | solution.py:41
  438.7 0.0 reduce-scatter.8.cloned.1.call-update
  438.7 95.0 %reduce-scatter.8.cloned.1.call-done = f32[16,32,128]{2,1,0:T(8,128)} async-done(((f32[512,32,128]{2,1,0:T(8,128)}), f32[16,32,128]{2,1,0:T(8,128)}) %reduce-scatter.8.cloned.1.call-update) | async-done | bytes 262160 | tf_op jit(solution)/shard_map/reduce_scatter | solution.py:42
  533.7 3.4 fusion.15
  (18 shorter events, 0.3 us)
Async XLA Ops:
  6.5 1.2 copy-start
  6.5 18.4 %copy-start.2 = (s32[1,1,192]{2,1,0:T(1,128)S(1)}, s32[1,1,192]{2,1,0:T(1,128)}, u32[]{:S(2)}) copy-start(s32[1,1,192]{2,1,0:T(1,128)} %param.8) | copy-start | bytes 2308
  6.5 18.4 %copy-start.3 = (s32[1,1,192]{2,1,0:T(1,128)S(1)}, s32[1,1,192]{2,1,0:T(1,128)}, u32[]{:S(2)}) copy-start(s32[1,1,192]{2,1,0:T(1,128)} %param.7) | copy-start | bytes 2308
  15.7 37.2 %all-to-all-start = ((bf16[1,128,32,128]{3,2,0,1:T(8,128)(2,1)}), bf16[1,128,32,128]{3,2,0,1:T(8,128)(2,1)S(1)}, u32[]{:S(2)}, u32[]{:S(2)}) async-start(bf16[1,128,32,128]{3,2,0,1:T(8,128)(2,1)} %bitcast.6), calls=%async_computation | async-start | bytes 2097152 | tf_op jit(solution)/shard_map/all_to_all | solution.py:11
  24.2 165.9 %reduce-scatter.4.cloned.1.call-start = ((), (), s32[]{:S(2)}) async-start(), calls=%async_computation.6 | async-start | bytes 8650752 | tf_op jit(solution)/shard_map/reduce_scatter | solution.py:42
  93.5 96.6 %copy-start.1 = (f32[1,16,32,128]{3,2,1,0:T(8,128)S(1)}, f32[1,16,32,128]{3,2,1,0:T(8,128)}, u32[]{:S(2)}) copy-start(f32[1,16,32,128]{3,2,1,0:T(8,128)} %param.11) | copy-start | bytes 786436
  93.5 268.4 %reduce-scatter.6.cloned.1.call-start = ((), (), s32[]{:S(2)}) async-start(), calls=%async_computation.7 | async-start | bytes 8650752 | tf_op jit(solution)/shard_map/reduce_scatter | solution.py:42
  267.0 266.6 %reduce-scatter.8.cloned.1.call-start = ((), (), s32[]{:S(2)}) async-start(), calls=%async_computation.8 | async-start | bytes 8650752 | tf_op jit(solution)/shard_map/reduce_scatter | solution.py:42
Sparse Core Ops, SparseCore 0:
  93.6 96.4 reduce-scatter.3
  267.2 94.6 reduce-scatter.5
  438.8 94.7 reduce-scatter.7
